TPU v7x, 512 devices: a whole 4x4x16 slice. The times are simulated.
512 devices in a mesh: hid: 64 (over y, x, z_hi, core), mod: 8 (over z_lo).
Axes of the slice: x: 4, y: 4, z: 16 (z_hi: 2, z_lo: 8; z = z_hi * 8 + z_lo), core: 2. Of those that a mesh axis runs over, the one named last changes fastest.
Arguments:
- tokens: bfloat16 [512, 8192], P('hid', 'mod'), may hold values from -6 to 6
- cotangent: bfloat16 [512, 8192], P('hid', 'mod'), may hold values from -1.2578125 to 1.2578125
- gate_weight: bfloat16 [8192, 26624], P('mod', 'hid'), may hold values from -0.0625 to 0.0625
- up_weight: bfloat16 [8192, 26624], P('mod', 'hid'), may hold values from -0.0625 to 0.0625
- down_weight: bfloat16 [26624, 8192], P('hid', 'mod'), may hold values from -0.0390625 to 0.0390625
Outputs:
- grad_in: bfloat16 [512, 8192], P('hid', 'mod')
- grad_gate: bfloat16 [8192, 26624], P('mod', 'hid')
- grad_up: bfloat16 [8192, 26624], P('mod', 'hid')
- grad_down: bfloat16 [26624, 8192], P('hid', 'mod')
All inputs are finite; a program needn't handle non-finite values.
Results may differ from a plain program's by a relative error of at most 0.027.
Values may be sent and summed in bfloat16 or wider, within the bound.
A program may use at most 64 MiB of HBM per device.

v0:
```python
import jax
import jax.numpy as jnp
from jax import lax
from jax.sharding import PartitionSpec as P

readout_scale = 2.0


def contract_last(left, right):
    return lax.dot_general(
        left, right, (((1,), (1,)), ((), ())), preferred_element_type=jnp.float32
    )


def contract_first(left, right):
    return lax.dot_general(
        left, right, (((0,), (0,)), ((), ())), preferred_element_type=jnp.float32
    )


def swiglu_grads(gate, up, back):
    back = readout_scale * back
    sigmoid_gate = jax.nn.sigmoid(gate)
    activated = gate * sigmoid_gate
    hidden = (activated * up).astype(jnp.bfloat16)
    d_gate = (back * up * sigmoid_gate * (1.0 + gate * (1.0 - sigmoid_gate))).astype(jnp.bfloat16)
    d_up = (back * activated).astype(jnp.bfloat16)
    return (hidden, d_gate, d_up)


def local(tokens, cotangent, gate_weight, up_weight, down_weight):
    piece = lax.all_gather(tokens, "hid", axis=0, tiled=True)
    token_rows = piece
    gate_part = jnp.dot(piece, gate_weight, preferred_element_type=jnp.float32)
    up_part = jnp.dot(piece, up_weight, preferred_element_type=jnp.float32)
    piece = lax.all_gather(cotangent, "hid", axis=0, tiled=True)
    back_part = contract_last(piece, down_weight)
    gate_sum, up_sum, back_sum = (
        lax.psum(gate_part.astype(jnp.bfloat16), "mod").astype(jnp.float32),
        lax.psum(up_part.astype(jnp.bfloat16), "mod").astype(jnp.float32),
        lax.psum(back_part.astype(jnp.bfloat16), "mod").astype(jnp.float32),
    )
    hidden, d_gate, d_up = swiglu_grads(gate_sum, up_sum, back_sum)
    grad_down = (readout_scale * contract_first(hidden, piece)).astype(jnp.bfloat16)
    grad_gate = contract_first(token_rows, d_gate).astype(jnp.bfloat16)
    grad_up = contract_first(token_rows, d_up).astype(jnp.bfloat16)
    grad_in = lax.psum_scatter(
        contract_last(d_gate, gate_weight) + contract_last(d_up, up_weight),
        "hid",
        scatter_dimension=0,
        tiled=True,
    ).astype(jnp.bfloat16)
    return (grad_in, grad_gate, grad_up, grad_down)


def solution(mesh):
    placed = (P("hid", "mod"), P("hid", "mod"), P("mod", "hid"), P("mod", "hid"), P("hid", "mod"))
    return jax.shard_map(
        local,
        mesh=mesh,
        in_specs=placed,
        out_specs=(P("hid", "mod"), P("mod", "hid"), P("mod", "hid"), P("hid", "mod")),
        check_vma=False,
    )
```

profile of v0, /device:TPU:1, one launch (start us, length us, event | category | flops | bytes accessed | tf_op | source)
XLA Modules:
  0.0 910.3 jit_solution(11970317265629496496)
XLA Ops:
  7.2 0.0 copy-start
  7.2 0.0 all-gather.5.cloned.1.call-start
  7.2 0.7 all-gather.5.cloned.1.call-update
  7.9 0.0 all-gather.3.cloned.1.call-start
  8.0 0.7 all-gather.3.cloned.1.call-update
  8.7 0.0 all-reduce.3.cloned.1.call-start
  8.7 113.0 %all-gather.5.cloned.1.call-done = bf16[512,1024]{1,0:T(8,128)(2,1)} async-done(((bf16[8,1024]{1,0:T(8,128)(2,1)}), bf16[512,1024]{1,0:T(8,128)(2,1)}) %all-gather.5.cloned.1.call-update) | async-done | bytes 1048592 | tf_op jit(solution)/shard_map/all_gather | solution.py:32
  121.7 0.0 copy-done
  121.7 2.8 convolution_convert_fusion.2
  124.4 0.0 copy-done.1
  124.4 0.0 copy-done.4
  124.4 1.4 convolution_convert_fusion.3
  125.8 92.6 %all-gather.3.cloned.1.call-done = bf16[512,1024]{1,0:T(8,128)(2,1)} async-done(((bf16[8,1024]{1,0:T(8,128)(2,1)}), bf16[512,1024]{1,0:T(8,128)(2,1)}) %all-gather.3.cloned.1.call-update) | async-done | bytes 1048592 | tf_op jit(solution)/shard_map/all_gather | solution.py:36
  218.5 0.0 copy-done.3
  218.5 2.6 convolution_convert_fusion.4
  221.1 0.0 all-reduce.3.cloned.1.call-update
  221.1 0.0 reduce-scatter.2.cloned.1.call-start
  221.2 115.0 %all-reduce.3.cloned.1.call-done = (bf16[512,416]{0,1:T(8,128)(2,1)}, bf16[512,416]{0,1:T(8,128)(2,1)}, bf16[512,416]{0,1:T(8,128)(2,1)}) async-done(((bf16[512,416]{0,1:T(8,128)(2,1)}, bf16[512,416]{0,1:T(8,128)(2,1)}, bf16[512,416]{0,1:T(8,128)(2,1)}), (bf16[512,416]{0,1:T(8,128)(2,1)}, bf16[512,416]{0,1:T(8,128)(2,1)}, bf16[512,416]{0,1:T(8,128)(2,1)})) %all-reduce.3.cloned.1.call-update) | async-done | bytes 1277968 | tf_op jit(solution)/shard_map/psum | solution.py:40
  336.2 2.3 fusion.13
  338.5 0.0 copy-done.5
  338.5 0.0 copy-done.7
  338.5 0.0 copy-done.8
  338.6 2.2 convolution_add_fusion
  340.7 0.0 reduce-scatter.2.cloned.1.call-update
  340.8 0.0 copy-start.2
  340.8 0.0 copy-start.6
  340.8 1.6 fusion.1
  342.4 0.0 copy-done.2
  342.4 1.6 multiply_convert_fusion
  344.0 1.7 fusion
  345.7 556.7 %reduce-scatter.2.cloned.1.call-done = f32[8,1024]{1,0:T(8,128)} async-done(((f32[512,1024]{1,0:T(8,128)}), f32[8,1024]{1,0:T(8,128)}) %reduce-scatter.2.cloned.1.call-update) | async-done | bytes 32784 | tf_op jit(solution)/shard_map/reduce_scatter | solution.py:47
  902.4 1.4 convert_element_type.53
  (7 shorter events, 0.0 us)
Async XLA Ops:
  7.2 114.5 %copy-start = (bf16[1024,416]{0,1:T(8,128)(2,1)S(1)}, bf16[1024,416]{0,1:T(8,128)(2,1)}, u32[]{:S(2)}) copy-start(bf16[1024,416]{0,1:T(8,128)(2,1)} %param.7) | copy-start | bytes 2555908
  7.2 114.5 %all-gather.5.cloned.1.call-start = ((), (), s32[]{:S(2)}) async-start(), calls=%async_computation.2 | async-start | bytes 1064960 | tf_op jit(solution)/shard_map/all_gather | solution.py:32
  7.9 210.5 %all-gather.3.cloned.1.call-start = ((), (), s32[]{:S(2)}) async-start(), calls=%async_computation.1 | async-start | bytes 1064960 | tf_op jit(solution)/shard_map/all_gather | solution.py:36
  8.7 327.5 %all-reduce.3.cloned.1.call-start = ((), (), s32[]{:S(2)}) async-start(), calls=%async_computation.4 | async-start | bytes 2555904 | tf_op jit(solution)/shard_map/psum | solution.py:40
  121.7 2.8 copy-start.1
  121.7 2.8 copy-start.4
  124.4 94.0 %copy-start.3 = (bf16[416,1024]{1,0:T(8,128)(2,1)S(1)}, bf16[416,1024]{1,0:T(8,128)(2,1)}, u32[]{:S(2)}) copy-start(bf16[416,1024]{1,0:T(8,128)(2,1)} %param.9) | copy-start | bytes 2555908
  221.1 681.3 %reduce-scatter.2.cloned.1.call-start = ((), (), s32[]{:S(2)}) async-start(), calls=%async_computation.3 | async-start | bytes 2129920 | tf_op jit(solution)/shard_map/reduce_scatter | solution.py:47
  336.2 2.4 copy-start.5
  336.2 2.4 copy-start.7
  336.2 2.4 copy-start.8
  340.8 1.6 copy-start.2
  340.8 1.6 copy-start.6
Sparse Core Ops, SparseCore 0:
  12.4 109.2 all-gather.4
  126.0 92.3 all-gather.2
  222.2 113.9 all-reduce.2
  340.9 561.4 reduce-scatter.1
where the time goes:
time: 923 us; the launch traced here: 910 us
  waiting for transfers between devices  879 us (95%)
  matrix products  16.2 us (2%)
  between operations  13.8 us (1%)
    reduce_scatter x1, waiting for transfers between devices, local(): lax.psum_scatter(contract_last(d_gate, gate_weight) + contract_last(d_up,...  557 us
    psum x1, waiting for transfers between devices, local(): lax.psum(up_part.astype(jnp.bfloat16), 'mod').astype(jnp.float32)  115 us
    all_gather x1, waiting for transfers between devices, local(): piece = lax.all_gather(tokens, 'hid', axis=0, tiled=True)  113 us
    all_gather x1, waiting for transfers between devices, local(): piece = lax.all_gather(cotangent, 'hid', axis=0, tiled=True)  92.6 us
  transfers between devices with their start and end apart: 4, of which 4 were waited for; matrix products, arithmetic and copies ran while one was open for 1% of the time, Pallas kernels for 0%

commit v1 on v0

v1 whole, which is shorter than its diff:
```python
import functools

import jax
import jax.numpy as jnp
from jax import lax
from jax.experimental import pallas as pl
from jax.experimental.pallas import tpu as pltpu
from jax.sharding import PartitionSpec as P

readout_scale = 2.0
N_MOD = 8
LAG = 2
ROWS = 32
MESH = pl.DeviceIdType.MESH
F32 = jnp.float32
BF16 = jnp.bfloat16


def swiglu_grads(gate, up, back):
    back = readout_scale * back
    sigmoid_gate = jax.nn.sigmoid(gate)
    activated = gate * sigmoid_gate
    hidden = (activated * up).astype(BF16)
    d_gate = (back * up * sigmoid_gate * (1.0 + gate * (1.0 - sigmoid_gate))).astype(BF16)
    d_up = (back * activated).astype(BF16)
    return hidden, d_gate, d_up


def kernel(
    tok_ref, cot_ref, wg_ref, wu_ref, wd_ref,
    gin_ref, gg_ref, gu_ref, gd_ref,
    xin, stage, full, wbuf, wt, part, redbuf, res, grad, sibbuf, rb1, a1, rb2, a2, rb3, outbuf, obuf,
    s0_send, s0_recv, ag_send, ag_recv, sib_send, sib_recv,
    red_send, red_recv, bc_send, bc_recv,
    r0_send, r0_recv, r1_send, r1_recv, r2_send, r2_recv, r3_send, r3_recv, r4_send, r4_recv,
    w_sem, o_sem,
):
    hid = lax.axis_index("hid")
    zl = lax.axis_index("mod")
    c = lax.rem(hid, 2)
    z = lax.rem(hid // 2, 2)
    x = lax.rem(hid // 4, 4)
    y = hid // 16
    chunks = part.shape[1]

    def dev(yy, xx, zz, cc):
        return (((yy * 4 + xx) * 2 + zz) * 2 + cc, zl)

    def coords(k_out, k_in):
        xx = lax.rem(x + k_in * (1 - c) + k_out * c, 4)
        yy = lax.rem(y + k_in * c + k_out * (1 - c), 4)
        return yy, xx

    def block(k_out, k_in):
        yy, xx = coords(k_out, k_in)
        return yy * 4 + xx

    def peer(k_out, k_in):
        yy, xx = coords(k_out, k_in)
        return dev(yy, xx, z, c)

    sibling = dev(y, x, z, 1 - c)

    def rcopy(src, dst, ssem, rsem, target):
        return pltpu.make_async_remote_copy(
            src_ref=src, dst_ref=dst, send_sem=ssem, recv_sem=rsem, device_id=target, device_id_type=MESH
        )

    w_copies = [
        pltpu.make_async_copy(wg_ref, wbuf.at[0], w_sem.at[0]),
        pltpu.make_async_copy(wu_ref, wbuf.at[1], w_sem.at[1]),
        pltpu.make_async_copy(wd_ref, wt.at[2], w_sem.at[2]),
    ]
    for copy in w_copies:
        copy.start()

    barrier = pltpu.get_barrier_semaphore()
    greeted = [sibling, dev(y, x, 1 - z, 0), dev(y, x, 1 - z, 1)]
    greeted += [peer(0, k) for k in (1, 2, 3)] + [peer(k, 0) for k in (1, 2, 3)]
    greeted += [(hid, lax.rem(zl + 1, N_MOD)), (hid, lax.rem(zl + N_MOD - 1, N_MOD))]
    for target in greeted:
        pl.semaphore_signal(barrier, inc=1, device_id=target, device_id_type=MESH)
    xin[0] = tok_ref[...]
    xin[1] = cot_ref[...]
    pl.semaphore_wait(barrier, len(greeted))

    slot = z * 2 + c
    first = [
        rcopy(xin.at[0], stage.at[slot], s0_send.at[0], s0_recv.at[slot], dev(y, x, 1 - z, 0)),
        rcopy(xin.at[1], stage.at[slot], s0_send.at[1], s0_recv.at[slot], dev(y, x, 1 - z, 1)),
        rcopy(xin.at[1 - c], stage.at[slot], s0_send.at[2], s0_recv.at[slot], sibling),
    ]
    for copy in first:
        copy.start()
    stage[slot] = xin[c]
    for other in (z * 2 + 1 - c, (1 - z) * 2, (1 - z) * 2 + 1):
        rcopy(xin.at[0], stage.at[other], s0_send.at[0], s0_recv.at[other], sibling).wait_recv()
    mine = y * 4 + x
    full[c, mine] = stage[...].astype(F32).reshape(32, stage.shape[2]).astype(BF16)

    def ag_copy(b, send_index, target):
        return rcopy(full.at[c, b], full.at[c, b], ag_send.at[send_index], ag_recv.at[b], target)

    def sib_copy(b):
        return rcopy(full.at[c, b], full.at[c, b], sib_send.at[b], sib_recv.at[b], sibling)

    for k in (1, 2, 3):
        ag_copy(mine, 12 + k - 1, peer(0, k)).start()
    for k in (1, 2, 3):
        ag_copy(mine, k - 1, peer(k, 0)).start()
    sib_copy(mine).start()

    for copy in w_copies:
        copy.wait()
    wt[0] = wbuf[0].T
    wt[1] = wbuf[1].T

    @pl.loop(1, 4)
    def _(k_in):
        b = block(0, 4 - k_in)
        ag_copy(b, 0, sibling).wait_recv()
        for k in (1, 2, 3):
            ag_copy(b, k_in * 3 + k - 1, peer(k, 0)).start()
        sib_copy(b).start()

    @pl.loop(0, 12)
    def _(j):
        b = block(4 - (1 + j % 3), lax.rem(4 - j // 3, 4))
        ag_copy(b, 0, sibling).wait_recv()
        sib_copy(b).start()

    @pl.loop(0, 16)
    def _(b):
        rcopy(full.at[1 - c, b], full.at[1 - c, b], sib_send.at[b], sib_recv.at[b], sibling).wait_recv()

    width = full.shape[3]
    for d in range(2):
        for i in range(3):
            acts = full[i // 2, d * 8:(d + 1) * 8].reshape(256, width)
            sums = lax.dot_general(wt[i], acts, (((1,), (1,)), ((), ())), preferred_element_type=F32)
            part[d, :, i] = sums.astype(BF16).reshape(chunks, ROWS, 256)

    last = N_MOD - 1

    def red_copy(d, k, target):
        return rcopy(part.at[d, k], redbuf.at[d, k], red_send.at[d, k], red_recv.at[d, k], (hid, target))

    def bc_copy(d, k, target):
        return rcopy(res.at[d, k], res.at[d, k], bc_send.at[d, k], bc_recv.at[d, k], (hid, target))

    @pl.loop(0, 2 * last * LAG + chunks)
    def _(step):
        for d in range(2):
            place = zl if d == 0 else last - zl
            ahead = jnp.minimum(zl + 1, last) if d == 0 else jnp.maximum(zl - 1, 0)
            behind = jnp.maximum(zl - 1, 0) if d == 0 else jnp.minimum(zl + 1, last)
            k = step - LAG * place
            live = (k >= 0) & (k < chunks)

            @pl.when(live & (place == 0))
            def _():
                red_copy(d, k, ahead).start()

            @pl.when(live & (place > 0) & (place < last))
            def _():
                red_copy(d, k, ahead).wait_recv()
                part[d, k] = (part[d, k].astype(F32) + redbuf[d, k].astype(F32)).astype(BF16)
                red_copy(d, k, ahead).start()

            @pl.when(live & (place == last))
            def _():
                red_copy(d, k, behind).wait_recv()
                sums = part[d, k].astype(F32) + redbuf[d, k].astype(F32)
                hidden, d_gate, d_up = swiglu_grads(sums[0], sums[1], sums[2])
                res[d, k, 0] = hidden
                res[d, k, 1] = d_gate
                res[d, k, 2] = d_up
                bc_copy(d, k, behind).start()

            kb = step - LAG * (2 * last - place)
            live_b = (kb >= 0) & (kb < chunks) & (place < last)

            @pl.when(live_b)
            def _():
                bc_copy(d, kb, behind).wait_recv()

                @pl.when(place > 0)
                def _():
                    bc_copy(d, kb, behind).start()

    half = width // 2
    hidden_units = chunks * ROWS

    def sib_grad(d):
        blocks = pl.ds(d * 8, 8)
        return rcopy(grad.at[1 - c, blocks], sibbuf.at[blocks], r0_send.at[d], r0_recv.at[d], sibling)

    for d in range(2):
        total = jnp.zeros((256, width), F32)
        for i in range(2):
            total += lax.dot_general(
                res[d, :, i + 1].reshape(hidden_units, 256), wt[i], (((0,), (0,)), ((), ())), preferred_element_type=F32
            )
        total = total.astype(BF16)
        for h in range(2):
            grad[h, d * 8:(d + 1) * 8] = total[:, h * half:(h + 1) * half].reshape(8, 32, half)
        sib_grad(d).start()

    def weight_grad(i, scale):
        total = jnp.zeros((hidden_units, width), F32)
        for d in range(2):
            acts = full[1 if i == 0 else 0, d * 8:(d + 1) * 8].reshape(256, width)
            total += jnp.dot(res[d, :, i].reshape(hidden_units, 256), acts, preferred_element_type=F32)
        if scale is not None:
            total = scale * total
        obuf[i] = total.astype(BF16)
        copy = pltpu.make_async_copy(obuf.at[i], (gd_ref, gg_ref, gu_ref)[i], o_sem.at[i])
        copy.start()
        return copy

    for d in range(2):
        sib_grad(d).wait_recv()
    for d in range(2):
        blocks = pl.ds(d * 8, 8)
        grad[c, blocks] = (grad[c, blocks].astype(F32) + sibbuf[blocks].astype(F32)).astype(BF16)

    def r1_copy(k_out, k_in):
        return rcopy(
            grad.at[c, block(k_out, k_in)], rb1.at[k_out - 1, k_in],
            r1_send.at[k_out - 1, k_in], r1_recv.at[k_out - 1, k_in], peer(k_out, 0),
        )

    def r2_copy(k_in):
        return rcopy(a1.at[k_in], rb2.at[k_in - 1], r2_send.at[k_in - 1], r2_recv.at[k_in - 1], peer(0, k_in))

    @pl.loop(1, 5)
    def _(j):
        k_in = lax.rem(j, 4)
        for k_out in (1, 2, 3):
            r1_copy(k_out, k_in).start()

    out_copies = [weight_grad(0, readout_scale)]

    for k_in in (1, 2, 3, 0):
        total = grad[c, block(0, k_in)].astype(F32)
        for k_out in (1, 2, 3):
            r1_copy(k_out, k_in).wait_recv()
        for k_out in (1, 2, 3):
            total += rb1[k_out - 1, k_in].astype(F32)
        a1[k_in] = total.astype(BF16)
        if k_in:
            r2_copy(k_in).start()

    out_copies.append(weight_grad(1, None))
    total = a1[0].astype(F32)
    for k_in in (1, 2, 3):
        r2_copy(k_in).wait_recv()
    for k_in in (1, 2, 3):
        total += rb2[k_in - 1].astype(F32)
    a2[...] = total.astype(BF16).reshape(2, 16, half)
    r3 = rcopy(a2.at[1 - z], rb3, r3_send, r3_recv, dev(y, x, 1 - z, c))
    r3.start()
    out_copies.append(weight_grad(2, None))
    r3.wait_recv()
    total = a2[z].astype(F32) + rb3[...].astype(F32)
    a3 = total.reshape(2, 8, half).astype(BF16)
    a1_out = outbuf
    a1_out[0] = a3
    r4 = rcopy(a1_out.at[0, 1 - c], a1_out.at[1, 0], r4_send, r4_recv, sibling)
    r4.start()
    r4.wait_recv()
    own = a1_out[0, c]
    theirs = a1_out[1, 0]
    is0 = c == 0
    gin_ref[:, :half] = jnp.where(is0, own, theirs)
    gin_ref[:, half:] = jnp.where(is0, theirs, own)

    for copy in first:
        copy.wait_send()

    @pl.loop(0, 15)
    def _(i):
        ag_copy(mine, i, sibling).wait_send()

    @pl.loop(0, 16)
    def _(b):
        sib_copy(b).wait_send()

    @pl.loop(0, chunks)
    def _(k):
        for d in range(2):
            place = zl if d == 0 else last - zl

            @pl.when(place < last)
            def _():
                red_copy(d, k, zl).wait_send()

            @pl.when(place > 0)
            def _():
                bc_copy(d, k, zl).wait_send()

    for d in range(2):
        sib_grad(d).wait_send()
    for k_in in range(4):
        for k_out in (1, 2, 3):
            r1_copy(k_out, k_in).wait_send()
        if k_in:
            r2_copy(k_in).wait_send()
    r3.wait_send()
    r4.wait_send()
    for copy in out_copies:
        copy.wait()


def local(tokens, cotangent, gate_weight, up_weight, down_weight):
    width = tokens.shape[1]
    units = down_weight.shape[0]
    chunks = units // ROWS
    half = width // 2
    dma = pltpu.SemaphoreType.DMA
    vmem = pl.BlockSpec(memory_space=pltpu.VMEM)
    hbm = pl.BlockSpec(memory_space=pl.ANY)
    grad_in, grad_gate, grad_up, grad_down = pl.pallas_call(
        kernel,
        out_shape=(
            jax.ShapeDtypeStruct(tokens.shape, BF16),
            jax.ShapeDtypeStruct((units, width), BF16),
            jax.ShapeDtypeStruct((units, width), BF16),
            jax.ShapeDtypeStruct((units, width), BF16),
        ),
        in_specs=[vmem, vmem, hbm, hbm, hbm],
        out_specs=(vmem, hbm, hbm, hbm),
        scratch_shapes=[
            pltpu.VMEM((2, 8, width), BF16),
            pltpu.VMEM((4, 8, width), BF16),
            pltpu.VMEM((2, 16, 32, width), BF16),
            pltpu.VMEM((2, width, units), BF16),
            pltpu.VMEM((3, units, width), BF16),
            pltpu.VMEM((2, chunks, 3, ROWS, 256), BF16),
            pltpu.VMEM((2, chunks, 3, ROWS, 256), BF16),
            pltpu.VMEM((2, chunks, 3, ROWS, 256), BF16),
            pltpu.VMEM((2, 16, 32, half), BF16),
            pltpu.VMEM((16, 32, half), BF16),
            pltpu.VMEM((3, 4, 32, half), BF16),
            pltpu.VMEM((4, 32, half), BF16),
            pltpu.VMEM((3, 32, half), BF16),
            pltpu.VMEM((2, 16, half), BF16),
            pltpu.VMEM((16, half), BF16),
            pltpu.VMEM((2, 2, 8, half), BF16),
            pltpu.VMEM((3, units, width), BF16),
            dma((3,)), dma((4,)), dma((15,)), dma((16,)), dma((16,)), dma((16,)),
            dma((2, chunks)), dma((2, chunks)), dma((2, chunks)), dma((2, chunks)),
            dma((2,)), dma((2,)), dma((3, 4)), dma((3, 4)), dma((3,)), dma((3,)),
            dma(()), dma(()), dma(()), dma(()),
            dma((3,)), dma((3,)),
        ],
        compiler_params=pltpu.CompilerParams(
            collective_id=0, has_side_effects=True, vmem_limit_bytes=48 * 1024 * 1024
        ),
    )(tokens, cotangent, gate_weight, up_weight, down_weight)
    return grad_in, grad_gate.T, grad_up.T, grad_down


def solution(mesh):
    placed = (P("hid", "mod"), P("hid", "mod"), P("mod", "hid"), P("mod", "hid"), P("hid", "mod"))
    return jax.shard_map(
        local,
        mesh=mesh,
        in_specs=placed,
        out_specs=(P("hid", "mod"), P("mod", "hid"), P("mod", "hid"), P("hid", "mod")),
        check_vma=False,
    )
```

time: 923 us -> 132 us (0.14); the launches traced: 910 us -> 131 us
  waiting for transfers between devices: 879 us -> 0 us
  Pallas kernels: 0 us -> 124 us
  matrix products: 16.2 us -> 0 us
  between operations: 13.8 us -> 0.7 us
    reduce_scatter x1 -> x0, waiting for transfers between devices: 557 us -> none  [local(): lax.psum_scatter(contract_last(d_gate, gate_weight) + contract_last(d_up,...]
    all_gather x2 -> x0, waiting for transfers between devices: 206 us -> none  [the longest x1 113 us: local(): piece = lax.all_gather(tokens, 'hid', axis=0, tiled=True)]
    pallas_call x0 -> x1, Pallas kernels: none -> 124 us  [local(): pl.pallas_call(kernel, out_shape=(jax.ShapeDtypeStruct(tokens.shape, BF16...]
    psum x1 -> x0, waiting for transfers between devices: 115 us -> none  [local(): lax.psum(up_part.astype(jnp.bfloat16), 'mod').astype(jnp.float32)]
    dot_general x8 -> x0, matrix products: 16.2 us -> none  [the longest x3 7.14 us: contract_last(): lax.dot_general(left, right, (((1,), (1,)), ((), ())), preferred_element_...]
  transfers between devices with their start and end apart: 4 -> 0, of which waited for: 4 -> 0; matrix products, arithmetic and copies ran while one was open for 1% -> 0% of each run, Pallas kernels for 0% -> 0%
where the time goes in v1:
time: 132 us; the launch traced here: 131 us
  Pallas kernels  124 us (94%)
  local copies, waits for them, and re-layouts  6.31 us (5%)
    pallas_call x1, Pallas kernels, local(): pl.pallas_call(kernel, out_shape=(jax.ShapeDtypeStruct(tokens.shape, BF16...  124 us
    unnamed x12, local copies, waits for them, and re-layouts  6.31 us

profile of v1, /device:TPU:1, one launch (start us, length us, event | category | flops | bytes accessed | tf_op | source)
XLA Modules:
  0.0 131.4 jit_solution(12646058449742726434)
XLA Ops:
  0.6 1.5 %copy.9.wg_ref = bf16[1024,416]{1,0:T(8,128)(2,1)S(1)} copy(bf16[1024,416]{0,1:T(8,128)(2,1)} %param.7) | data formatting | bytes 1703936 | tf_op args[2]
  2.1 0.0 copy-start
  2.1 0.0 copy-start.1
  2.1 0.0 copy-start.2
  2.1 1.5 %copy.10.wu_ref = bf16[1024,416]{1,0:T(8,128)(2,1)S(1)} copy(bf16[1024,416]{0,1:T(8,128)(2,1)} %param.8) | data formatting | bytes 1703936 | tf_op args[3]
  3.7 0.0 copy-done
  3.7 0.0 copy-done.1
  3.7 0.0 copy-done.2
  3.7 124.4 %shard_map.84 = (bf16[8,1024]{1,0:T(8,128)(2,1)S(1)}, bf16[416,1024]{1,0:T(8,128)(2,1)S(1)}, bf16[416,1024]{1,0:T(8,128)(2,1)S(1)}, bf16[416,1024]{1,0:T(8,128)(2,1)S(1)}) custom-call(bf16[8,1024]{1,0:T(8,128)(2,1)S(1)} %copy-done.1, bf16[8,1024]{1,0:T(8,128)(2,1)S(1)} %copy-done.2, bf16[1024,416]{1,0:T(8,128)(2,1)S(1)} %copy.9.wg_ref, ...), custom_call_target="tpu_custom_call" | custom-call | tf_op jit(solution)/shard_map/pallas_call | solution.py:323
  128.1 0.6 copy.15
  128.7 0.9 copy.16
  129.6 0.9 copy.17
  130.5 0.9 copy.18
Async XLA Ops:
  2.1 1.6 %copy-start = (bf16[416,1024]{1,0:T(8,128)(2,1)S(1)}, bf16[416,1024]{1,0:T(8,128)(2,1)}, u32[]{:S(2)}) copy-start(bf16[416,1024]{1,0:T(8,128)(2,1)} %wd_ref.1) | copy-start | bytes 2555908
  2.1 1.6 %copy-start.1 = (bf16[8,1024]{1,0:T(8,128)(2,1)S(1)}, bf16[8,1024]{1,0:T(8,128)(2,1)}, u32[]{:S(2)}) copy-start(bf16[8,1024]{1,0:T(8,128)(2,1)} %tok_ref.1) | copy-start | bytes 49156
  2.1 1.6 %copy-start.2 = (bf16[8,1024]{1,0:T(8,128)(2,1)S(1)}, bf16[8,1024]{1,0:T(8,128)(2,1)}, u32[]{:S(2)}) copy-start(bf16[8,1024]{1,0:T(8,128)(2,1)} %cot_ref.1) | copy-start | bytes 49156

commit v2 on v1

v2 whole, which is shorter than its diff:
```python
import functools

import jax
import jax.numpy as jnp
from jax import lax
from jax.experimental import pallas as pl
from jax.experimental.pallas import tpu as pltpu
from jax.sharding import PartitionSpec as P

readout_scale = 2.0
N_MOD = 8
LAG = 6
ROWS = 32
MESH = pl.DeviceIdType.MESH
F32 = jnp.float32
BF16 = jnp.bfloat16


def swiglu_grads(gate, up, back):
    back = readout_scale * back
    sigmoid_gate = jax.nn.sigmoid(gate)
    activated = gate * sigmoid_gate
    hidden = (activated * up).astype(BF16)
    d_gate = (back * up * sigmoid_gate * (1.0 + gate * (1.0 - sigmoid_gate))).astype(BF16)
    d_up = (back * activated).astype(BF16)
    return hidden, d_gate, d_up


def kernel(
    tok_ref, cot_ref, wg_ref, wu_ref, wd_ref,
    gin_ref, gg_ref, gu_ref, gd_ref,
    xin, stage, full, wt, part, redbuf, res, grad, sibbuf, rb1, a1, rb2, a2, rb3, outbuf, obuf,
    s0_send, s0_recv, ag_send, ag_recv, sib_send, sib_recv,
    red_send, red_recv, bc_send, bc_recv,
    r0_send, r0_recv, r1_send, r1_recv, r2_send, r2_recv, r3_send, r3_recv, r4_send, r4_recv,
    w_sem, o_sem,
):
    hid = lax.axis_index("hid")
    zl = lax.axis_index("mod")
    c = lax.rem(hid, 2)
    z = lax.rem(hid // 2, 2)
    x = lax.rem(hid // 4, 4)
    y = hid // 16
    chunks = part.shape[1]
    last = N_MOD - 1

    def dev(yy, xx, zz, cc):
        return (((yy * 4 + xx) * 2 + zz) * 2 + cc, zl)

    def coords(k_out, k_in):
        xx = lax.rem(x + k_in * (1 - c) + k_out * c, 4)
        yy = lax.rem(y + k_in * c + k_out * (1 - c), 4)
        return yy, xx

    def block(k_out, k_in):
        yy, xx = coords(k_out, k_in)
        return yy * 4 + xx

    def peer(k_out, k_in):
        yy, xx = coords(k_out, k_in)
        return dev(yy, xx, z, c)

    def quarter(q):
        return pl.ds(lax.rem(y + q, 4) * 4, 4)

    sibling = dev(y, x, z, 1 - c)

    def rcopy(src, dst, ssem, rsem, target):
        return pltpu.make_async_remote_copy(
            src_ref=src, dst_ref=dst, send_sem=ssem, recv_sem=rsem, device_id=target, device_id_type=MESH
        )

    barrier = pltpu.get_barrier_semaphore()
    greeted = [sibling, dev(y, x, 1 - z, 0), dev(y, x, 1 - z, 1)]
    greeted += [peer(0, k) for k in (1, 2, 3)] + [peer(k, 0) for k in (1, 2, 3)]
    for target in greeted:
        pl.semaphore_signal(barrier, inc=1, device_id=target, device_id_type=MESH)

    @pl.when(zl < last)
    def _():
        pl.semaphore_signal(barrier, inc=1, device_id=(hid, jnp.minimum(zl + 1, last)), device_id_type=MESH)

    @pl.when(zl > 0)
    def _():
        pl.semaphore_signal(barrier, inc=1, device_id=(hid, jnp.maximum(zl - 1, 0)), device_id_type=MESH)

    w_copies = [
        pltpu.make_async_copy(wg_ref, wt.at[0], w_sem.at[0]),
        pltpu.make_async_copy(wu_ref, wt.at[1], w_sem.at[1]),
        pltpu.make_async_copy(wd_ref, wt.at[2], w_sem.at[2]),
    ]
    for copy in w_copies:
        copy.start()
    xin[0] = tok_ref[...]
    xin[1] = cot_ref[...]
    pl.semaphore_wait(barrier, len(greeted) + jnp.minimum(zl, 1) + jnp.minimum(last - zl, 1))

    slot = z * 2 + c
    first = [
        rcopy(xin.at[0], stage.at[slot], s0_send.at[0], s0_recv.at[slot], dev(y, x, 1 - z, 0)),
        rcopy(xin.at[1], stage.at[slot], s0_send.at[1], s0_recv.at[slot], dev(y, x, 1 - z, 1)),
        rcopy(xin.at[1 - c], stage.at[slot], s0_send.at[2], s0_recv.at[slot], sibling),
    ]
    for copy in first:
        copy.start()
    stage[slot] = xin[c]
    for other in (z * 2 + 1 - c, (1 - z) * 2, (1 - z) * 2 + 1):
        rcopy(xin.at[0], stage.at[other], s0_send.at[0], s0_recv.at[other], sibling).wait_recv()
    mine = y * 4 + x
    full[c, mine] = stage[...].astype(F32).reshape(32, stage.shape[2]).astype(BF16)

    def ag_copy(b, target):
        return rcopy(full.at[c, b], full.at[c, b], ag_send, ag_recv.at[b], target)

    def sib_copy(b):
        return rcopy(full.at[c, b], full.at[c, b], sib_send, sib_recv.at[b], sibling)

    for k in (1, 2, 3):
        ag_copy(mine, peer(0, k)).start()
    for k in (1, 2, 3):
        ag_copy(mine, peer(k, 0)).start()
    sib_copy(mine).start()

    for k_in in (1, 3, 2):
        b = block(0, k_in)
        ag_copy(b, sibling).wait_recv()
        for k in (1, 3, 2):
            ag_copy(b, peer(k, 0)).start()
        sib_copy(b).start()

    def gather_rows(q):
        @pl.loop(0, 4)
        def _(i):
            k_out = q * (1 - c) + i * c

            @pl.when(k_out > 0)
            def _():
                b = block(k_out, i * (1 - c) + q * c)
                ag_copy(b, sibling).wait_recv()
                sib_copy(b).start()

    def sibling_rows(q):
        @pl.loop(0, 4)
        def _(i):
            b = lax.rem(y + q, 4) * 4 + i
            rcopy(full.at[1 - c, b], full.at[1 - c, b], sib_send, sib_recv.at[b], sibling).wait_recv()

    width = full.shape[3]
    hidden_units = chunks * ROWS

    def partial_sums(q):
        for i in range(3):
            acts = full[i // 2, quarter(q)].reshape(128, width)
            sums = lax.dot_general(wt[i], acts, (((1,), (1,)), ((), ())), preferred_element_type=F32)
            part[q, :, i] = sums.astype(BF16).reshape(chunks, ROWS, 128)

    roots = (last, 0, last // 2, last // 2 + 1)

    def red_copy(q, k, side, target):
        return rcopy(part.at[q, k], redbuf.at[side, q, k], red_send.at[q], red_recv.at[side, q, k], (hid, target))

    def bc_copy(q, k, side, target):
        return rcopy(res.at[q, k], res.at[q, k], bc_send.at[side, q], bc_recv.at[q, k], (hid, target))

    def chain_step(step, which):
        for q in which:
            root = roots[q]
            stride = 1 if q < 2 else 2
            base = 0 if q < 2 else chunks
            below = zl < root
            far = (zl == 0) | (zl == last)
            onward = jnp.clip(jnp.where(below, zl + 1, zl - 1), 0, last)
            outward = jnp.clip(jnp.where(below, zl - 1, zl + 1), 0, last)
            side = jnp.where(below, 0, 1)
            root_lag = LAG * max(root, last - root)
            at = step - base - jnp.where(zl == root, root_lag, LAG * jnp.where(below, zl, last - zl))
            k = at // stride
            live = (at >= 0) & (at < chunks * stride) & (lax.rem(at, stride) == 0)

            @pl.when(live & (zl != root))
            def _():
                @pl.when(jnp.logical_not(far))
                def _():
                    red_copy(q, k, side, onward).wait_recv()
                    part[q, k] = (part[q, k].astype(F32) + redbuf[side, q, k].astype(F32)).astype(BF16)

                red_copy(q, k, side, onward).start()

            @pl.when(live & (zl == root))
            def _():
                sums = part[q, k].astype(F32)
                if root > 0:
                    red_copy(q, k, 0, root).wait_recv()
                    sums += redbuf[0, q, k].astype(F32)
                if root < last:
                    red_copy(q, k, 1, root).wait_recv()
                    sums += redbuf[1, q, k].astype(F32)
                hidden, d_gate, d_up = swiglu_grads(sums[0], sums[1], sums[2])
                res[q, k, 0] = hidden
                res[q, k, 1] = d_gate
                res[q, k, 2] = d_up
                if root > 0:
                    bc_copy(q, k, 0, root - 1).start()
                if root < last:
                    bc_copy(q, k, 1, root + 1).start()

            at_b = step - base - root_lag - LAG * jnp.where(below, root - zl, zl - root)
            kb = at_b // stride

            @pl.when((at_b >= 0) & (at_b < chunks * stride) & (lax.rem(at_b, stride) == 0) & (zl != root))
            def _():
                bc_copy(q, kb, 0, zl).wait_recv()

                @pl.when(jnp.logical_not(far))
                def _():
                    bc_copy(q, kb, side, outward).start()

    def chain_steps(start, stop, which):
        @pl.loop(start, stop)
        def _(step):
            chain_step(step, which)

    gather_rows(0)
    gather_rows(1)
    for copy in w_copies:
        copy.wait()
    sibling_rows(0)
    partial_sums(0)
    sibling_rows(1)
    partial_sums(1)
    chain_steps(0, LAG, (0, 1))
    gather_rows(2)
    gather_rows(3)
    chain_steps(LAG, chunks, (0, 1))
    for q in (2, 3):
        sibling_rows(q)
        partial_sums(q)
    chain_steps(chunks, max(chunks + 2 * last * LAG, 3 * chunks + (last + 1) * LAG), (0, 1, 2, 3))

    half = width // 2

    def sib_grad(q):
        return rcopy(
            grad.at[1 - c, quarter(q)], sibbuf.at[quarter(q)], r0_send.at[q], r0_recv.at[q], sibling
        )

    def columns(i, qs):
        return jnp.concatenate([res[q, :, i].reshape(hidden_units, 128) for q in qs], axis=1)

    for qs in ((0, 1), (2, 3)):
        total = jnp.zeros((256, width), F32)
        for i in range(2):
            total += lax.dot_general(columns(i + 1, qs), wt[i], (((0,), (0,)), ((), ())), preferred_element_type=F32)
        total = total.astype(BF16)
        for j, q in enumerate(qs):
            for h in range(2):
                grad[h, quarter(q)] = total[j * 128:(j + 1) * 128, h * half:(h + 1) * half].reshape(4, 32, half)
            sib_grad(q).start()

    def weight_grad(i, scale):
        acts = jnp.concatenate([full[1 if i == 0 else 0, quarter(q)].reshape(128, width) for q in range(4)], axis=0)
        total = jnp.dot(columns(i, range(4)), acts, preferred_element_type=F32)
        if scale is not None:
            total = scale * total
        obuf[i] = total.astype(BF16)
        copy = pltpu.make_async_copy(obuf.at[i], (gd_ref, gg_ref, gu_ref)[i], o_sem.at[i])
        copy.start()
        return copy

    def r1_copy(k_out, k_in):
        return rcopy(
            grad.at[c, block(k_out, k_in)], rb1.at[k_out - 1, k_in],
            r1_send, r1_recv.at[k_out - 1, k_in], peer(k_out, 0),
        )

    def r2_copy(k_in):
        return rcopy(a1.at[k_in], rb2.at[k_in - 1], r2_send, r2_recv.at[k_in - 1], peer(0, k_in))

    for q in range(4):
        rows = quarter(q)
        sib_grad(q).wait_recv()
        grad[c, rows] = (grad[c, rows].astype(F32) + sibbuf[rows].astype(F32)).astype(BF16)

        @pl.loop(0, 4)
        def _(i):
            k_out = q * (1 - c) + i * c

            @pl.when(k_out > 0)
            def _():
                r1_copy(k_out, i * (1 - c) + q * c).start()

    out_copies = [weight_grad(0, readout_scale)]

    for k_in in (1, 2, 3, 0):
        total = grad[c, block(0, k_in)].astype(F32)
        for k_out in (1, 2, 3):
            r1_copy(k_out, k_in).wait_recv()
        for k_out in (1, 2, 3):
            total += rb1[k_out - 1, k_in].astype(F32)
        a1[k_in] = total.astype(BF16)
        if k_in:
            r2_copy(k_in).start()

    out_copies.append(weight_grad(1, None))
    total = a1[0].astype(F32)
    for k_in in (1, 2, 3):
        r2_copy(k_in).wait_recv()
    for k_in in (1, 2, 3):
        total += rb2[k_in - 1].astype(F32)
    a2[...] = total.astype(BF16).reshape(2, 16, half)
    r3 = rcopy(a2.at[1 - z], rb3, r3_send, r3_recv, dev(y, x, 1 - z, c))
    r3.start()
    out_copies.append(weight_grad(2, None))

    for copy in first:
        copy.wait_send()
    rows = pl.ds(0, 15)
    rcopy(full.at[c, rows], full.at[c, rows], ag_send, ag_recv.at[0], sibling).wait_send()
    rcopy(full.at[c], full.at[c], sib_send, sib_recv.at[0], sibling).wait_send()
    for q in range(4):
        root = roots[q]

        @pl.when(zl != root)
        def _():
            rcopy(part.at[q], redbuf.at[0, q], red_send.at[q], red_recv.at[0, q, 0], sibling).wait_send()

        for side in range(2):
            sends = ((zl <= root) & (zl > 0)) if side == 0 else ((zl >= root) & (zl < last))

            @pl.when(sends)
            def _():
                rcopy(res.at[q], res.at[q], bc_send.at[side, q], bc_recv.at[q, 0], sibling).wait_send()

        sib_grad(q).wait_send()
    rows = pl.ds(0, 12)
    rcopy(grad.at[c, rows], sibbuf.at[rows], r1_send, r1_recv.at[0, 0], sibling).wait_send()
    rcopy(rb2, rb2, r2_send, r2_recv.at[0], sibling).wait_send()
    for copy in out_copies:
        copy.wait()

    r3.wait_recv()
    total = a2[z].astype(F32) + rb3[...].astype(F32)
    outbuf[0] = total.reshape(2, 8, half).astype(BF16)
    r4 = rcopy(outbuf.at[0, 1 - c], outbuf.at[1, 0], r4_send, r4_recv, sibling)
    r4.start()
    own = outbuf[0, c]
    r4.wait_recv()
    theirs = outbuf[1, 0]
    is0 = c == 0
    gin_ref[:, :half] = jnp.where(is0, own, theirs)
    gin_ref[:, half:] = jnp.where(is0, theirs, own)
    r3.wait_send()
    r4.wait_send()


def local(tokens, cotangent, gate_weight, up_weight, down_weight):
    width = tokens.shape[1]
    units = down_weight.shape[0]
    chunks = units // ROWS
    half = width // 2
    dma = pltpu.SemaphoreType.DMA
    vmem = pl.BlockSpec(memory_space=pltpu.VMEM)
    hbm = pl.BlockSpec(memory_space=pl.ANY)
    grad_in, grad_gate, grad_up, grad_down = pl.pallas_call(
        kernel,
        out_shape=(
            jax.ShapeDtypeStruct(tokens.shape, BF16),
            jax.ShapeDtypeStruct((units, width), BF16),
            jax.ShapeDtypeStruct((units, width), BF16),
            jax.ShapeDtypeStruct((units, width), BF16),
        ),
        in_specs=[vmem, vmem, hbm, hbm, hbm],
        out_specs=(vmem, hbm, hbm, hbm),
        scratch_shapes=[
            pltpu.VMEM((2, 8, width), BF16),
            pltpu.VMEM((4, 8, width), BF16),
            pltpu.VMEM((2, 16, 32, width), BF16),
            pltpu.VMEM((3, units, width), BF16),
            pltpu.VMEM((4, chunks, 3, ROWS, 128), BF16),
            pltpu.VMEM((2, 4, chunks, 3, ROWS, 128), BF16),
            pltpu.VMEM((4, chunks, 3, ROWS, 128), BF16),
            pltpu.VMEM((2, 16, 32, half), BF16),
            pltpu.VMEM((16, 32, half), BF16),
            pltpu.VMEM((3, 4, 32, half), BF16),
            pltpu.VMEM((4, 32, half), BF16),
            pltpu.VMEM((3, 32, half), BF16),
            pltpu.VMEM((2, 16, half), BF16),
            pltpu.VMEM((16, half), BF16),
            pltpu.VMEM((2, 2, 8, half), BF16),
            pltpu.VMEM((3, units, width), BF16),
            dma((3,)), dma((4,)), dma(()), dma((16,)), dma(()), dma((16,)),
            dma((4,)), dma((2, 4, chunks)), dma((2, 4)), dma((4, chunks)),
            dma((4,)), dma((4,)), dma(()), dma((3, 4)), dma(()), dma((3,)),
            dma(()), dma(()), dma(()), dma(()),
            dma((3,)), dma((3,)),
        ],
        compiler_params=pltpu.CompilerParams(
            collective_id=0, has_side_effects=True, vmem_limit_bytes=56 * 1024 * 1024
        ),
    )(tokens, cotangent, gate_weight.T, up_weight.T, down_weight)
    return grad_in, grad_gate.T, grad_up.T, grad_down


def solution(mesh):
    placed = (P("hid", "mod"), P("hid", "mod"), P("mod", "hid"), P("mod", "hid"), P("hid", "mod"))
    return jax.shard_map(
        local,
        mesh=mesh,
        in_specs=placed,
        out_specs=(P("hid", "mod"), P("mod", "hid"), P("mod", "hid"), P("hid", "mod")),
        check_vma=False,
    )
```

time: 132 us -> 123 us (0.932)
  Pallas kernels: 124 us -> 116 us
    pallas_call x1, Pallas kernels: 124 us -> 116 us  [local(): pl.pallas_call(kernel, out_shape=(jax.ShapeDtypeStruct(tokens.shape, BF16...]
    unnamed x12 -> x8, local copies, waits for them, and re-layouts: 6.31 us -> 5.88 us
where the time goes in v2:
time: 123 us; the launch traced here: 122 us
  Pallas kernels  116 us (94%)
  local copies, waits for them, and re-layouts  5.88 us (5%)
    pallas_call x1, Pallas kernels, local(): pl.pallas_call(kernel, out_shape=(jax.ShapeDtypeStruct(tokens.shape, BF16...  116 us
    unnamed x8, local copies, waits for them, and re-layouts  5.88 us

profile of v2, /device:TPU:1, one launch (start us, length us, event | category | flops | bytes accessed | tf_op | source)
XLA Modules:
  0.0 122.3 jit_solution(4334620011361494141)
XLA Ops:
  0.6 115.8 %shard_map.84 = (bf16[8,1024]{1,0:T(8,128)(2,1)}, bf16[416,1024]{1,0:T(8,128)(2,1)}, bf16[416,1024]{1,0:T(8,128)(2,1)}, bf16[416,1024]{1,0:T(8,128)(2,1)}) custom-call(bf16[8,1024]{1,0:T(8,128)(2,1)} %tok_ref.1, bf16[8,1024]{1,0:T(8,128)(2,1)} %cot_ref.1, bf16[416,1024]{1,0:T(8,128)(2,1)} %bitcast.4, bf16[416,1024]{1,0:T(8,128)(2,1)} %bitcast.5, ...), custom_call_target="tpu_custom_call" | custom-call | tf_op jit(solution)/shard_map/pallas_call | solution.py:364
  116.4 1.3 %copy.13 = bf16[8,1024]{1,0:T(8,128)(2,1)} copy(bf16[8,1024]{1,0:T(8,128)(2,1)} %get-tuple-element.16) | data formatting | bytes 32768
  117.7 0.0 copy-start.1
  117.7 2.2 %copy.14 = bf16[1024,416]{0,1:T(8,128)(2,1)} copy(bf16[1024,416]{0,1:T(8,128)(2,1)} %bitcast.7) | data formatting | bytes 1703936
  119.9 0.0 copy-done.1
  119.9 0.0 copy-start
  119.9 0.9 copy.15
  120.8 0.6 copy-done
  121.4 0.9 copy.16
Async XLA Ops:
  117.7 2.2 %copy-start.1 = (bf16[416,1024]{1,0:T(8,128)(2,1)S(1)}, bf16[416,1024]{1,0:T(8,128)(2,1)}, u32[]{:S(2)}) copy-start(bf16[416,1024]{1,0:T(8,128)(2,1)} %get-tuple-element.10) | copy-start | bytes 2555908
  119.9 1.5 %copy-start = (bf16[416,1024]{1,0:T(8,128)(2,1)S(1)}, bf16[416,1024]{1,0:T(8,128)(2,1)}, u32[]{:S(2)}) copy-start(bf16[416,1024]{1,0:T(8,128)(2,1)} %get-tuple-element.19) | copy-start | bytes 2555908

commit v3 on v2

--- a/solution.py
+++ b/solution.py
@@ -60,8 +60,14 @@
         yy, xx = coords(k_out, k_in)
         return dev(yy, xx, z, c)
 
+    def half_of(q):
+        return z if q < 2 else 1 - z
+
     def quarter(q):
-        return pl.ds(lax.rem(y + q, 4) * 4, 4)
+        return pl.ds(half_of(q) * 16 + (q % 2) * 8, 8)
+
+    def blocks_of(q):
+        return pl.ds((q % 2) * 8, 8)
 
     sibling = dev(y, x, z, 1 - c)
 
@@ -97,17 +103,14 @@
 
     slot = z * 2 + c
     first = [
+        rcopy(xin.at[1 - c], stage.at[slot], s0_send.at[2], s0_recv.at[slot], sibling),
         rcopy(xin.at[0], stage.at[slot], s0_send.at[0], s0_recv.at[slot], dev(y, x, 1 - z, 0)),
         rcopy(xin.at[1], stage.at[slot], s0_send.at[1], s0_recv.at[slot], dev(y, x, 1 - z, 1)),
-        rcopy(xin.at[1 - c], stage.at[slot], s0_send.at[2], s0_recv.at[slot], sibling),
     ]
     for copy in first:
         copy.start()
     stage[slot] = xin[c]
-    for other in (z * 2 + 1 - c, (1 - z) * 2, (1 - z) * 2 + 1):
-        rcopy(xin.at[0], stage.at[other], s0_send.at[0], s0_recv.at[other], sibling).wait_recv()
     mine = y * 4 + x
-    full[c, mine] = stage[...].astype(F32).reshape(32, stage.shape[2]).astype(BF16)
 
     def ag_copy(b, target):
         return rcopy(full.at[c, b], full.at[c, b], ag_send, ag_recv.at[b], target)
@@ -115,35 +118,43 @@
     def sib_copy(b):
         return rcopy(full.at[c, b], full.at[c, b], sib_send, sib_recv.at[b], sibling)
 
-    for k in (1, 2, 3):
-        ag_copy(mine, peer(0, k)).start()
-    for k in (1, 2, 3):
-        ag_copy(mine, peer(k, 0)).start()
-    sib_copy(mine).start()
-
-    for k_in in (1, 3, 2):
-        b = block(0, k_in)
-        ag_copy(b, sibling).wait_recv()
+    def arrived(other):
+        rcopy(xin.at[0], stage.at[other], s0_send.at[0], s0_recv.at[other], sibling).wait_recv()
+
+    def begin_half(zz):
+        b = zz * 16 + mine
+        rows = stage[pl.ds(zz * 2, 2)].astype(F32)
+        full[c, b] = rows.reshape(16, stage.shape[2]).astype(BF16)
+        for k in (1, 3, 2):
+            ag_copy(b, peer(0, k)).start()
         for k in (1, 3, 2):
             ag_copy(b, peer(k, 0)).start()
         sib_copy(b).start()
 
-    def gather_rows(q):
+    def inner_half(zz):
+        for k_in in (1, 3, 2):
+            b = zz * 16 + block(0, k_in)
+            ag_copy(b, sibling).wait_recv()
+            for k in (1, 3, 2):
+                ag_copy(b, peer(k, 0)).start()
+            sib_copy(b).start()
+
+    def outer_half(zz):
         @pl.loop(0, 4)
-        def _(i):
-            k_out = q * (1 - c) + i * c
-
-            @pl.when(k_out > 0)
-            def _():
-                b = block(k_out, i * (1 - c) + q * c)
+        def _(k_in):
+            for k_out in (1, 3, 2):
+                b = zz * 16 + block(k_out, k_in)
                 ag_copy(b, sibling).wait_recv()
                 sib_copy(b).start()
 
-    def sibling_rows(q):
-        @pl.loop(0, 4)
+    def sibling_half(zz):
+        @pl.loop(0, 16)
         def _(i):
-            b = lax.rem(y + q, 4) * 4 + i
+            b = zz * 16 + i
             rcopy(full.at[1 - c, b], full.at[1 - c, b], sib_send, sib_recv.at[b], sibling).wait_recv()
+
+    width = full.shape[3]
+    hidden_units = chunks * ROWS
 
     width = full.shape[3]
     hidden_units = chunks * ROWS
@@ -220,42 +231,48 @@
         def _(step):
             chain_step(step, which)
 
-    gather_rows(0)
-    gather_rows(1)
+    arrived(z * 2 + 1 - c)
+    begin_half(z)
+    inner_half(z)
+    arrived((1 - z) * 2)
+    arrived((1 - z) * 2 + 1)
+    begin_half(1 - z)
+    outer_half(z)
+    sibling_half(z)
+    inner_half(1 - z)
     for copy in w_copies:
         copy.wait()
-    sibling_rows(0)
     partial_sums(0)
-    sibling_rows(1)
     partial_sums(1)
     chain_steps(0, LAG, (0, 1))
-    gather_rows(2)
-    gather_rows(3)
+    outer_half(1 - z)
     chain_steps(LAG, chunks, (0, 1))
-    for q in (2, 3):
-        sibling_rows(q)
-        partial_sums(q)
+    sibling_half(1 - z)
+    partial_sums(2)
+    partial_sums(3)
     chain_steps(chunks, max(chunks + 2 * last * LAG, 3 * chunks + (last + 1) * LAG), (0, 1, 2, 3))
 
     half = width // 2
 
     def sib_grad(q):
         return rcopy(
-            grad.at[1 - c, quarter(q)], sibbuf.at[quarter(q)], r0_send.at[q], r0_recv.at[q], sibling
+            grad.at[1 - c, blocks_of(q)], sibbuf.at[blocks_of(q)], r0_send.at[q], r0_recv.at[q], sibling
         )
 
     def columns(i, qs):
         return jnp.concatenate([res[q, :, i].reshape(hidden_units, 128) for q in qs], axis=1)
 
-    for qs in ((0, 1), (2, 3)):
+    for qs in ((0, 2), (1, 3)):
         total = jnp.zeros((256, width), F32)
         for i in range(2):
             total += lax.dot_general(columns(i + 1, qs), wt[i], (((0,), (0,)), ((), ())), preferred_element_type=F32)
         total = total.astype(BF16)
         for j, q in enumerate(qs):
             for h in range(2):
-                grad[h, quarter(q)] = total[j * 128:(j + 1) * 128, h * half:(h + 1) * half].reshape(4, 32, half)
-            sib_grad(q).start()
+                grad[h, blocks_of(q), half_of(q)] = (
+                    total[j * 128:(j + 1) * 128, h * half:(h + 1) * half].reshape(8, 16, half)
+                )
+        sib_grad(qs[0]).start()
 
     def weight_grad(i, scale):
         acts = jnp.concatenate([full[1 if i == 0 else 0, quarter(q)].reshape(128, width) for q in range(4)], axis=0)
@@ -276,18 +293,14 @@
     def r2_copy(k_in):
         return rcopy(a1.at[k_in], rb2.at[k_in - 1], r2_send, r2_recv.at[k_in - 1], peer(0, k_in))
 
-    for q in range(4):
-        rows = quarter(q)
+    for q in range(2):
+        rows = blocks_of(q)
         sib_grad(q).wait_recv()
         grad[c, rows] = (grad[c, rows].astype(F32) + sibbuf[rows].astype(F32)).astype(BF16)
 
-        @pl.loop(0, 4)
-        def _(i):
-            k_out = q * (1 - c) + i * c
-
-            @pl.when(k_out > 0)
-            def _():
-                r1_copy(k_out, i * (1 - c) + q * c).start()
+    for k_in in (1, 2, 3, 0):
+        for k_out in (1, 2, 3):
+            r1_copy(k_out, k_in).start()
 
     out_copies = [weight_grad(0, readout_scale)]
 
@@ -307,14 +320,14 @@
         r2_copy(k_in).wait_recv()
     for k_in in (1, 2, 3):
         total += rb2[k_in - 1].astype(F32)
-    a2[...] = total.astype(BF16).reshape(2, 16, half)
+    a2[...] = total.astype(BF16)
     r3 = rcopy(a2.at[1 - z], rb3, r3_send, r3_recv, dev(y, x, 1 - z, c))
     r3.start()
     out_copies.append(weight_grad(2, None))
 
     for copy in first:
         copy.wait_send()
-    rows = pl.ds(0, 15)
+    rows = pl.ds(0, 30)
     rcopy(full.at[c, rows], full.at[c, rows], ag_send, ag_recv.at[0], sibling).wait_send()
     rcopy(full.at[c], full.at[c], sib_send, sib_recv.at[0], sibling).wait_send()
     for q in range(4):
@@ -331,6 +344,7 @@
             def _():
                 rcopy(res.at[q], res.at[q], bc_send.at[side, q], bc_recv.at[q, 0], sibling).wait_send()
 
+    for q in range(2):
         sib_grad(q).wait_send()
     rows = pl.ds(0, 12)
     rcopy(grad.at[c, rows], sibbuf.at[rows], r1_send, r1_recv.at[0, 0], sibling).wait_send()
@@ -374,28 +388,28 @@
         scratch_shapes=[
             pltpu.VMEM((2, 8, width), BF16),
             pltpu.VMEM((4, 8, width), BF16),
-            pltpu.VMEM((2, 16, 32, width), BF16),
+            pltpu.VMEM((2, 32, 16, width), BF16),
             pltpu.VMEM((3, units, width), BF16),
             pltpu.VMEM((4, chunks, 3, ROWS, 128), BF16),
             pltpu.VMEM((2, 4, chunks, 3, ROWS, 128), BF16),
             pltpu.VMEM((4, chunks, 3, ROWS, 128), BF16),
-            pltpu.VMEM((2, 16, 32, half), BF16),
-            pltpu.VMEM((16, 32, half), BF16),
-            pltpu.VMEM((3, 4, 32, half), BF16),
-            pltpu.VMEM((4, 32, half), BF16),
-            pltpu.VMEM((3, 32, half), BF16),
+            pltpu.VMEM((2, 16, 2, 16, half), BF16),
+            pltpu.VMEM((16, 2, 16, half), BF16),
+            pltpu.VMEM((3, 4, 2, 16, half), BF16),
+            pltpu.VMEM((4, 2, 16, half), BF16),
+            pltpu.VMEM((3, 2, 16, half), BF16),
             pltpu.VMEM((2, 16, half), BF16),
             pltpu.VMEM((16, half), BF16),
             pltpu.VMEM((2, 2, 8, half), BF16),
             pltpu.VMEM((3, units, width), BF16),
-            dma((3,)), dma((4,)), dma(()), dma((16,)), dma(()), dma((16,)),
+            dma((3,)), dma((4,)), dma(()), dma((32,)), dma(()), dma((32,)),
             dma((4,)), dma((2, 4, chunks)), dma((2, 4)), dma((4, chunks)),
-            dma((4,)), dma((4,)), dma(()), dma((3, 4)), dma(()), dma((3,)),
+            dma((2,)), dma((2,)), dma(()), dma((3, 4)), dma(()), dma((3,)),
             dma(()), dma(()), dma(()), dma(()),
             dma((3,)), dma((3,)),
         ],
         compiler_params=pltpu.CompilerParams(
-            collective_id=0, has_side_effects=True, vmem_limit_bytes=56 * 1024 * 1024
+            collective_id=0, has_side_effects=True, vmem_limit_bytes=50 * 1024 * 1024
         ),
     )(tokens, cotangent, gate_weight.T, up_weight.T, down_weight)
     return grad_in, grad_gate.T, grad_up.T, grad_down

time: 123 us -> 111 us (0.902)
  Pallas kernels: 116 us -> 104 us
    pallas_call x1, Pallas kernels: 116 us -> 104 us  [local(): pl.pallas_call(kernel, out_shape=(jax.ShapeDtypeStruct(tokens.shape, BF16...]
    unnamed x8 -> x10, local copies, waits for them, and re-layouts: 5.88 us -> 5.89 us
where the time goes in v3:
time: 111 us
  Pallas kernels  104 us (94%)
  local copies, waits for them, and re-layouts  5.89 us (5%)
    pallas_call x1, Pallas kernels, local(): pl.pallas_call(kernel, out_shape=(jax.ShapeDtypeStruct(tokens.shape, BF16...  104 us
    unnamed x10, local copies, waits for them, and re-layouts  5.89 us

profile of v3, /device:TPU:1, one launch (start us, length us, event | category | flops | bytes accessed | tf_op | source)
XLA Modules:
  0.0 110.9 jit_solution(8659955077371770469)
XLA Ops:
  0.6 0.0 copy-start
  0.6 1.1 %copy-done = bf16[1024,416]{0,1:T(8,128)(2,1)S(1)} copy-done((bf16[1024,416]{0,1:T(8,128)(2,1)S(1)}, bf16[1024,416]{0,1:T(8,128)(2,1)}, u32[]{:S(2)}) %copy-start) | copy-done | bytes 851992
  1.8 0.0 copy-start.1
  1.8 0.7 copy-done.1
  2.5 0.0 copy-start.2
  2.5 0.7 copy-done.2
  3.2 104.4 %shard_map.84 = (bf16[8,1024]{1,0:T(8,128)(2,1)S(1)}, bf16[416,1024]{1,0:T(8,128)(2,1)S(1)}, bf16[416,1024]{1,0:T(8,128)(2,1)S(1)}, bf16[416,1024]{1,0:T(8,128)(2,1)S(1)}) custom-call(bf16[8,1024]{1,0:T(8,128)(2,1)S(1)} %copy-done.1, bf16[8,1024]{1,0:T(8,128)(2,1)S(1)} %copy-done.2, bf16[416,1024]{1,0:T(8,128)(2,1)S(1)} %bitcast.4, ...), custom_call_target="tpu_custom_call" | custom-call | tf_op jit(solution)/shard_map/pallas_call | solution.py:378
  107.6 0.6 copy.13
  108.2 0.9 copy.14
  109.1 0.9 copy.15
  110.0 0.9 copy.16
Async XLA Ops:
  0.6 1.2 %copy-start = (bf16[1024,416]{0,1:T(8,128)(2,1)S(1)}, bf16[1024,416]{0,1:T(8,128)(2,1)}, u32[]{:S(2)}) copy-start(bf16[1024,416]{0,1:T(8,128)(2,1)} %param.7) | copy-start | bytes 2555908
  1.8 0.7 copy-start.1
  2.5 0.7 copy-start.2

commit v4 on v3

--- a/solution.py
+++ b/solution.py
@@ -29,10 +29,10 @@
 def kernel(
     tok_ref, cot_ref, wg_ref, wu_ref, wd_ref,
     gin_ref, gg_ref, gu_ref, gd_ref,
-    xin, stage, full, wt, part, redbuf, res, grad, sibbuf, rb1, a1, rb2, a2, rb3, outbuf, obuf,
+    xin, stage, full, wt, part, redbuf, res, grad, sibbuf, rb1, a1, rb2, a2, rb3, obuf,
     s0_send, s0_recv, ag_send, ag_recv, sib_send, sib_recv,
     red_send, red_recv, bc_send, bc_recv,
-    r0_send, r0_recv, r1_send, r1_recv, r2_send, r2_recv, r3_send, r3_recv, r4_send, r4_recv,
+    r0_send, r0_recv, r1_send, r1_recv, r2_send, r2_recv, r3_send, r3_recv,
     w_sem, o_sem,
 ):
     hid = lax.axis_index("hid")
@@ -76,6 +76,18 @@
             src_ref=src, dst_ref=dst, send_sem=ssem, recv_sem=rsem, device_id=target, device_id_type=MESH
         )
 
+    x_copies = [
+        pltpu.make_async_copy(tok_ref, xin.at[0], w_sem.at[3]),
+        pltpu.make_async_copy(cot_ref, xin.at[1], w_sem.at[4]),
+    ]
+    w_copies = [
+        pltpu.make_async_copy(wg_ref, wt.at[0], w_sem.at[0]),
+        pltpu.make_async_copy(wu_ref, wt.at[1], w_sem.at[1]),
+        pltpu.make_async_copy(wd_ref, wt.at[2], w_sem.at[2]),
+    ]
+    for copy in x_copies + w_copies:
+        copy.start()
+
     barrier = pltpu.get_barrier_semaphore()
     greeted = [sibling, dev(y, x, 1 - z, 0), dev(y, x, 1 - z, 1)]
     greeted += [peer(0, k) for k in (1, 2, 3)] + [peer(k, 0) for k in (1, 2, 3)]
@@ -90,15 +102,8 @@
     def _():
         pl.semaphore_signal(barrier, inc=1, device_id=(hid, jnp.maximum(zl - 1, 0)), device_id_type=MESH)
 
-    w_copies = [
-        pltpu.make_async_copy(wg_ref, wt.at[0], w_sem.at[0]),
-        pltpu.make_async_copy(wu_ref, wt.at[1], w_sem.at[1]),
-        pltpu.make_async_copy(wd_ref, wt.at[2], w_sem.at[2]),
-    ]
-    for copy in w_copies:
-        copy.start()
-    xin[0] = tok_ref[...]
-    xin[1] = cot_ref[...]
+    for copy in x_copies:
+        copy.wait()
     pl.semaphore_wait(barrier, len(greeted) + jnp.minimum(zl, 1) + jnp.minimum(last - zl, 1))
 
     slot = z * 2 + c
@@ -298,9 +303,15 @@
         sib_grad(q).wait_recv()
         grad[c, rows] = (grad[c, rows].astype(F32) + sibbuf[rows].astype(F32)).astype(BF16)
 
-    for k_in in (1, 2, 3, 0):
-        for k_out in (1, 2, 3):
-            r1_copy(k_out, k_in).start()
+        @pl.loop(q * 8, q * 8 + 8)
+        def _(b):
+            dy = lax.rem(b // 4 + 4 - y, 4)
+            dx = lax.rem(lax.rem(b, 4) + 4 - x, 4)
+            k_out = dy * (1 - c) + dx * c
+
+            @pl.when(k_out > 0)
+            def _():
+                r1_copy(k_out, dx * (1 - c) + dy * c).start()
 
     out_copies = [weight_grad(0, readout_scale)]
 
@@ -320,9 +331,15 @@
         r2_copy(k_in).wait_recv()
     for k_in in (1, 2, 3):
         total += rb2[k_in - 1].astype(F32)
-    a2[...] = total.astype(BF16)
-    r3 = rcopy(a2.at[1 - z], rb3, r3_send, r3_recv, dev(y, x, 1 - z, c))
-    r3.start()
+    a2[...] = total.reshape(4, 8, half).astype(BF16)
+    finals = [
+        rcopy(a2.at[(1 - z) * 2], rb3.at[c, 1], r3_send.at[0], r3_recv.at[c, 1], dev(y, x, 1 - z, 0)),
+        rcopy(a2.at[(1 - z) * 2 + 1], rb3.at[c, 1], r3_send.at[1], r3_recv.at[c, 1], dev(y, x, 1 - z, 1)),
+        rcopy(a2.at[z * 2 + 1 - c], rb3.at[c, 0], r3_send.at[2], r3_recv.at[c, 0], sibling),
+    ]
+    for copy in finals:
+        copy.start()
+    rb3[c, 0] = a2[z * 2 + c]
     out_copies.append(weight_grad(2, None))
 
     for copy in first:
@@ -352,19 +369,13 @@
     for copy in out_copies:
         copy.wait()
 
-    r3.wait_recv()
-    total = a2[z].astype(F32) + rb3[...].astype(F32)
-    outbuf[0] = total.reshape(2, 8, half).astype(BF16)
-    r4 = rcopy(outbuf.at[0, 1 - c], outbuf.at[1, 0], r4_send, r4_recv, sibling)
-    r4.start()
-    own = outbuf[0, c]
-    r4.wait_recv()
-    theirs = outbuf[1, 0]
-    is0 = c == 0
-    gin_ref[:, :half] = jnp.where(is0, own, theirs)
-    gin_ref[:, half:] = jnp.where(is0, theirs, own)
-    r3.wait_send()
-    r4.wait_send()
+    for h, source in ((1 - c, 0), (0, 1), (1, 1)):
+        rcopy(a2.at[0], rb3.at[h, source], r3_send.at[0], r3_recv.at[h, source], sibling).wait_recv()
+    for h in range(2):
+        total = rb3[h, 0].astype(F32) + rb3[h, 1].astype(F32)
+        gin_ref[:, h * half:(h + 1) * half] = total.astype(BF16)
+    for copy in finals:
+        copy.wait_send()
 
 
 def local(tokens, cotangent, gate_weight, up_weight, down_weight):
@@ -383,7 +394,7 @@
             jax.ShapeDtypeStruct((units, width), BF16),
             jax.ShapeDtypeStruct((units, width), BF16),
         ),
-        in_specs=[vmem, vmem, hbm, hbm, hbm],
+        in_specs=[hbm] * 5,
         out_specs=(vmem, hbm, hbm, hbm),
         scratch_shapes=[
             pltpu.VMEM((2, 8, width), BF16),
@@ -398,20 +409,19 @@
             pltpu.VMEM((3, 4, 2, 16, half), BF16),
             pltpu.VMEM((4, 2, 16, half), BF16),
             pltpu.VMEM((3, 2, 16, half), BF16),
-            pltpu.VMEM((2, 16, half), BF16),
-            pltpu.VMEM((16, half), BF16),
+            pltpu.VMEM((4, 8, half), BF16),
             pltpu.VMEM((2, 2, 8, half), BF16),
             pltpu.VMEM((3, units, width), BF16),
             dma((3,)), dma((4,)), dma(()), dma((32,)), dma(()), dma((32,)),
             dma((4,)), dma((2, 4, chunks)), dma((2, 4)), dma((4, chunks)),
             dma((2,)), dma((2,)), dma(()), dma((3, 4)), dma(()), dma((3,)),
-            dma(()), dma(()), dma(()), dma(()),
-            dma((3,)), dma((3,)),
+            dma((3,)), dma((2, 2)),
+            dma((5,)), dma((3,)),
         ],
         compiler_params=pltpu.CompilerParams(
             collective_id=0, has_side_effects=True, vmem_limit_bytes=50 * 1024 * 1024
         ),
-    )(tokens, cotangent, gate_weight.T, up_weight.T, down_weight)
+    )(*(pltpu.with_memory_space_constraint(a, pltpu.HBM) for a in (tokens, cotangent, gate_weight.T, up_weight.T, down_weight)))
     return grad_in, grad_gate.T, grad_up.T, grad_down
 
 

time: 111 us -> 108 us (0.973)
  local copies, waits for them, and re-layouts: 5.89 us -> 3.31 us
    unnamed x10 -> x4, local copies, waits for them, and re-layouts: 5.89 us -> 3.31 us
where the time goes in v4:
time: 108 us
  Pallas kernels  104 us (96%)
  local copies, waits for them, and re-layouts  3.31 us (3%)
    pallas_call x1, Pallas kernels, local(): pl.pallas_call(kernel, out_shape=(jax.ShapeDtypeStruct(tokens.shape, BF16...  104 us
    unnamed x4, local copies, waits for them, and re-layouts  3.31 us

profile of v4, /device:TPU:1, one launch (start us, length us, event | category | flops | bytes accessed | tf_op | source)
XLA Modules:
  0.0 108.2 jit_solution(17574071653054806431)
XLA Ops:
  0.6 104.2 %shard_map.84 = (bf16[8,1024]{1,0:T(8,128)(2,1)S(1)}, bf16[416,1024]{1,0:T(8,128)(2,1)S(1)}, bf16[416,1024]{1,0:T(8,128)(2,1)S(1)}, bf16[416,1024]{1,0:T(8,128)(2,1)S(1)}) custom-call(bf16[8,1024]{1,0:T(8,128)(2,1)} %tok_ref.1, bf16[8,1024]{1,0:T(8,128)(2,1)} %cot_ref.1, bf16[416,1024]{1,0:T(8,128)(2,1)} %bitcast.6, bf16[416,1024]{1,0:T(8,128)(2,1)} %bitcast.7, ...), custom_call_target="tpu_custom_call" | custom-call | tf_op jit(solution)/shard_map/pallas_call | solution.py:389
  104.9 0.6 copy.13
  105.5 0.9 copy.14
  106.4 0.9 copy.15
  107.3 0.9 copy.16

commit v5 on v4

--- a/solution.py
+++ b/solution.py
@@ -244,14 +244,15 @@
     begin_half(1 - z)
     outer_half(z)
     sibling_half(z)
-    inner_half(1 - z)
     for copy in w_copies:
         copy.wait()
     partial_sums(0)
     partial_sums(1)
-    chain_steps(0, LAG, (0, 1))
+    chain_steps(0, LAG // 2, (0, 1))
+    inner_half(1 - z)
+    chain_steps(LAG // 2, LAG + 2, (0, 1))
     outer_half(1 - z)
-    chain_steps(LAG, chunks, (0, 1))
+    chain_steps(LAG + 2, chunks, (0, 1))
     sibling_half(1 - z)
     partial_sums(2)
     partial_sums(3)
@@ -325,7 +326,6 @@
         if k_in:
             r2_copy(k_in).start()
 
-    out_copies.append(weight_grad(1, None))
     total = a1[0].astype(F32)
     for k_in in (1, 2, 3):
         r2_copy(k_in).wait_recv()
@@ -340,6 +340,7 @@
     for copy in finals:
         copy.start()
     rb3[c, 0] = a2[z * 2 + c]
+    out_copies.append(weight_grad(1, None))
     out_copies.append(weight_grad(2, None))
 
     for copy in first:

time: 108 us -> 107 us (level)
    pallas_call x1, Pallas kernels: 104 us -> 103 us  [local(): pl.pallas_call(kernel, out_shape=(jax.ShapeDtypeStruct(tokens.shape, BF16...]
where the time goes in v5:
time: 107 us
  Pallas kernels  103 us (96%)
  local copies, waits for them, and re-layouts  3.31 us (3%)
    pallas_call x1, Pallas kernels, local(): pl.pallas_call(kernel, out_shape=(jax.ShapeDtypeStruct(tokens.shape, BF16...  103 us
    unnamed x4, local copies, waits for them, and re-layouts  3.31 us

profile of v5, /device:TPU:1, one launch (start us, length us, event | category | flops | bytes accessed | tf_op | source)
XLA Modules:
  0.0 107.1 jit_solution(5991974505118120270)
XLA Ops:
  0.6 103.1 %shard_map.84 = (bf16[8,1024]{1,0:T(8,128)(2,1)S(1)}, bf16[416,1024]{1,0:T(8,128)(2,1)S(1)}, bf16[416,1024]{1,0:T(8,128)(2,1)S(1)}, bf16[416,1024]{1,0:T(8,128)(2,1)S(1)}) custom-call(bf16[8,1024]{1,0:T(8,128)(2,1)} %tok_ref.1, bf16[8,1024]{1,0:T(8,128)(2,1)} %cot_ref.1, bf16[416,1024]{1,0:T(8,128)(2,1)} %bitcast.6, bf16[416,1024]{1,0:T(8,128)(2,1)} %bitcast.7, ...), custom_call_target="tpu_custom_call" | custom-call | tf_op jit(solution)/shard_map/pallas_call | solution.py:390
  103.8 0.6 copy.13
  104.4 0.9 copy.14
  105.3 0.9 copy.15
  106.2 0.9 copy.16
